TPU v7x, 32 devices: a whole 2x2x4 slice. The times are simulated.
32 devices in a mesh: head: 2 (over x), tok: 16 (over z, y, core).
Axes of the slice: x: 2, y: 2, z: 4, core: 2. Of those that a mesh axis runs over, the one named last changes fastest.
Arguments:
- queries: bfloat16 [3072, 1024], P('tok', 'head'), may hold values from -512 to 512
- keys: bfloat16 [3072, 1024], P('tok', 'head'), may hold values from -8 to 8
- values: bfloat16 [3072, 1024], P('tok', 'head'), may hold values from -6 to 6
- out_grad: bfloat16 [3072, 1024], P('tok', 'head'), may hold values from -6 to 6
- w_query: bfloat16 [1024, 1024], P(None, 'head'), may hold values from -0.1875 to 0.1875
- w_key: bfloat16 [1024, 1024], P(None, 'head'), may hold values from -0.1875 to 0.1875
- w_value: bfloat16 [1024, 1024], P(None, 'head'), may hold values from -0.1875 to 0.1875
- w_out: bfloat16 [1024, 1024], P('head'), may hold values from -0.1875 to 0.1875
- page_cluster: int32 [96], replicated, may hold values from 0 to 15, as said below
Outputs:
- input_grad: bfloat16 [3072, 1024], P('tok', 'head')
Inputs may be any that keep to these rules, and one draw needn't show every extreme that they name: `page_cluster`: the 6 pages k * 6 to k * 6 + 5, for each k, name distinct clusters. No cluster is named by more than 8 pages, and some cluster by exactly 8.
All inputs are finite; a program needn't handle non-finite values.
Results may differ from a plain program's by a relative error of at most 0.014.
Values may be sent and summed in bfloat16 or wider, within the bound.
A program may use at most 64 MiB of HBM per device.

v0:
```python
import jax
import jax.numpy as jnp
from jax import lax
from jax.sharding import PartitionSpec as P

HEAD_DIM = 128
PAGE = 32


def per_device(queries, keys, values, out_grad, w_query, w_key, w_value, w_out, page_cluster):
    tok_rows, head_cols = queries.shape
    pages_here = tok_rows // PAGE
    heads_here = head_cols // HEAD_DIM
    peers = lax.axis_size("tok")
    myself = lax.axis_index("tok")
    page_total = page_cluster.shape[0]
    slot_count = peers // 2
    cluster_rows = slot_count * PAGE
    score_scale = HEAD_DIM ** (-0.5)
    grad_heads = jnp.einsum(
        "td,hd->th",
        lax.all_gather(out_grad, "head", axis=1, tiled=True),
        w_out,
        preferred_element_type=jnp.float32,
    ).astype(jnp.bfloat16)
    page_order = jnp.arange(page_total, dtype=jnp.int32)
    peer_order = jnp.arange(peers, dtype=jnp.int32)
    cluster_onehot = (page_cluster[:, None] == peer_order[None, :]).astype(jnp.int32)
    running_count = jnp.cumsum(cluster_onehot, axis=0) - cluster_onehot
    page_rank = jnp.sum(running_count * cluster_onehot, axis=1)
    my_clusters = lax.dynamic_slice_in_dim(page_cluster, myself * pages_here, pages_here)
    going = my_clusters[None, :] == peer_order[:, None]
    going_any = jnp.any(going, axis=1)
    going_index = jnp.sum(
        going.astype(jnp.int32) * jnp.arange(pages_here, dtype=jnp.int32)[None, :], axis=1
    )

    def outgoing(matrix):
        paged = matrix.reshape(pages_here, PAGE, matrix.shape[1])
        picked = jnp.take(paged, going_index, axis=0)
        return jnp.where(going_any[:, None, None], picked, jnp.zeros_like(picked))

    arrived = (
        lax.all_to_all(outgoing(queries), "tok", split_axis=0, concat_axis=0, tiled=True),
        lax.all_to_all(outgoing(keys), "tok", split_axis=0, concat_axis=0, tiled=True),
        lax.all_to_all(outgoing(values), "tok", split_axis=0, concat_axis=0, tiled=True),
        lax.all_to_all(outgoing(grad_heads), "tok", split_axis=0, concat_axis=0, tiled=True),
    )
    slot_order = jnp.arange(slot_count, dtype=jnp.int32)
    slot_hit = (page_cluster[None, :] == myself) & (page_rank[None, :] == slot_order[:, None])
    filled = jnp.any(slot_hit, axis=1)
    slot_page = jnp.sum(slot_hit.astype(jnp.int32) * page_order[None, :], axis=1)
    slot_source = slot_page // pages_here

    def assemble(matrix):
        picked = jnp.take(matrix, slot_source, axis=0)
        picked = jnp.where(filled[:, None, None], picked, jnp.zeros_like(picked))
        return picked.reshape(cluster_rows, heads_here, HEAD_DIM)

    slot_query = assemble(arrived[0])
    slot_keys = assemble(arrived[1])
    slot_values = assemble(arrived[2])
    slot_grads = assemble(arrived[3])
    inner_index = jnp.arange(PAGE, dtype=jnp.int32)
    key_pos = (slot_page[:, None] * PAGE + inner_index[None, :]).reshape(cluster_rows)
    key_live = jnp.broadcast_to(filled[:, None], (slot_count, PAGE)).reshape(cluster_rows)
    key_order = jnp.arange(cluster_rows, dtype=jnp.int32)
    block_rows = min(512, cluster_rows)
    dkey_sum = jnp.zeros((cluster_rows, heads_here, HEAD_DIM), jnp.float32)
    dvalue_sum = jnp.zeros((cluster_rows, heads_here, HEAD_DIM), jnp.float32)
    query_parts = []
    for block_index in range(cluster_rows // block_rows):
        first_row = block_index * block_rows
        last_row = first_row + block_rows
        part_query = slot_query[first_row:last_row]
        part_grads = slot_grads[first_row:last_row]
        row_pos = key_pos[first_row:last_row]
        row_order = key_order[first_row:last_row]
        allowed = key_live[None, :] & (key_pos[None, :] <= row_pos[:, None]) | (
            key_order[None, :] == row_order[:, None]
        )
        score = (
            jnp.einsum("qhd,khd->hqk", part_query, slot_keys, preferred_element_type=jnp.float32)
            * score_scale
        )
        score = jnp.where(allowed[None], score, -1e30)
        row_max = jnp.max(score, axis=2, keepdims=True)
        raised = jnp.where(allowed[None], jnp.exp(score - row_max), 0.0)
        weights = raised / jnp.sum(raised, axis=2, keepdims=True)
        weights_half = weights.astype(jnp.bfloat16)
        grad_weights = jnp.einsum(
            "qhd,khd->hqk", part_grads, slot_values, preferred_element_type=jnp.float32
        )
        row_delta = jnp.sum(weights * grad_weights, axis=2, keepdims=True)
        grad_score = (weights * (grad_weights - row_delta)).astype(jnp.bfloat16)
        grad_query = (
            jnp.einsum("hqk,khd->qhd", grad_score, slot_keys, preferred_element_type=jnp.float32)
            * score_scale
        )
        query_parts.append(grad_query.astype(jnp.bfloat16))
        dkey_sum = dkey_sum + jnp.einsum(
            "hqk,qhd->khd", grad_score, part_query, preferred_element_type=jnp.float32
        )
        dvalue_sum = dvalue_sum + jnp.einsum(
            "hqk,qhd->khd", weights_half, part_grads, preferred_element_type=jnp.float32
        )
    slot_dquery = jnp.concatenate(query_parts, axis=0).reshape(cluster_rows, head_cols)
    slot_dkey = (dkey_sum * score_scale).astype(jnp.bfloat16).reshape(cluster_rows, head_cols)
    slot_dvalue = dvalue_sum.astype(jnp.bfloat16).reshape(cluster_rows, head_cols)
    back_hit = (slot_source[None, :] == peer_order[:, None]) & filled[None, :]
    back_any = jnp.any(back_hit, axis=1)
    back_slot = jnp.sum(back_hit.astype(jnp.int32) * slot_order[None, :], axis=1)
    share_rows = w_query.shape[0] // lax.axis_size("head")
    total = jnp.einsum("dh,th->dt", w_query, slot_dquery, preferred_element_type=jnp.float32)
    total = total + jnp.einsum("dh,th->dt", w_key, slot_dkey, preferred_element_type=jnp.float32)
    total = total + jnp.einsum(
        "dh,th->dt", w_value, slot_dvalue, preferred_element_type=jnp.float32
    )
    column_share = lax.psum_scatter(
        total.astype(jnp.bfloat16), "head", scatter_dimension=0, tiled=True
    )
    column_share = column_share.reshape(share_rows, slot_count, PAGE)
    picked = jnp.take(column_share, back_slot, axis=1)
    picked = jnp.where(back_any[None, :, None], picked, jnp.zeros_like(picked))
    returned = lax.all_to_all(picked, "tok", split_axis=1, concat_axis=1, tiled=True)
    input_grad = jnp.take(returned, my_clusters, axis=1).reshape(share_rows, tok_rows).T
    return input_grad


def solution(mesh):
    placed = (
        P("tok", "head"),
        P("tok", "head"),
        P("tok", "head"),
        P("tok", "head"),
        P(None, "head"),
        P(None, "head"),
        P(None, "head"),
        P("head", None),
        P(),
    )
    return jax.shard_map(
        per_device, mesh=mesh, in_specs=placed, out_specs=P("tok", "head"), check_vma=False
    )
```

profile of v0, /device:TPU:0, one launch (start us, length us, event | category | flops | bytes accessed | tf_op | source)
XLA Modules:
  0.0 150.0 jit_solution(11652533963918098453)
XLA Ops:
  6.5 0.8 compare_and_fusion.3
  7.6 8.8 %all_gather.3 = bf16[192,1024]{1,0:T(8,128)(2,1)S(1)} all-gather(bf16[192,512]{1,0:T(8,128)(2,1)} %param.16), channel_id=1, replica_groups=mesh['head'=2,'tok'=16] {'head'}, dimensions={1}, use_global_device_ids=true | all-gather | bytes 589824 | tf_op jit(solution)/shard_map/all_gather | solution.py:22
  16.3 1.8 %convolution_convert_fusion.1 = bf16[192,512]{1,0:T(8,128)(2,1)S(1)} fusion(bf16[192,1024]{1,0:T(8,128)(2,1)S(1)} %all_gather.3, bf16[512,1024]{1,0:T(8,128)(2,1)} %param.20), kind=kOutput, calls=%fused_computation.25 | convolution fusion | flops 201424896 | bytes 1638400 | tf_op jit(solution)/shard_map/td,hd->th/dot_general | solution.py:20
  18.1 0.6 gather_fusion.6
  18.7 0.6 gather_fusion.2
  19.3 0.6 gather_fusion.4
  19.9 0.6 gather_fusion.8
  20.5 1.3 select_select_fusion.2
  21.8 20.2 %all_to_all.25 = bf16[16,32,512]{2,1,0:T(8,128)(2,1)S(1)} all-to-all(bf16[16,32,512]{2,1,0:T(8,128)(2,1)S(1)} %get-tuple-element.18), channel_id=1, replica_groups=mesh['head'=2,'tok'=16] {'tok'}, dimensions={0} | all-to-all | bytes 1048576 | tf_op jit(solution)/shard_map/all_to_all | solution.py:45
  42.0 18.4 %all_to_all.26 = bf16[16,32,512]{2,1,0:T(8,128)(2,1)S(1)} all-to-all(bf16[16,32,512]{2,1,0:T(8,128)(2,1)S(1)} %get-tuple-element.16), channel_id=1, replica_groups=mesh['head'=2,'tok'=16] {'tok'}, dimensions={0} | all-to-all | bytes 1048576 | tf_op jit(solution)/shard_map/all_to_all | solution.py:47
  60.4 4.2 %all-to-all-start.3 = ((bf16[16,32,512]{2,1,0:T(8,128)(2,1)}), bf16[16,32,512]{2,1,0:T(8,128)(2,1)S(1)}, u32[]{:S(2)}, u32[]{:S(2)}) async-start(bf16[16,32,512]{2,1,0:T(8,128)(2,1)} %get-tuple-element.17), calls=%async_computation.3 | async-start | bytes 1048576 | tf_op jit(solution)/shard_map/all_to_all | solution.py:46
  65.4 13.4 %all-to-all-done.3 = bf16[16,32,512]{2,1,0:T(8,128)(2,1)S(1)} async-done(((bf16[16,32,512]{2,1,0:T(8,128)(2,1)}), bf16[16,32,512]{2,1,0:T(8,128)(2,1)S(1)}, u32[]{:S(2)}, u32[]{:S(2)}) %all-to-all-start.3) | async-done | bytes 524320 | tf_op jit(solution)/shard_map/all_to_all | solution.py:46
  78.8 4.2 %all-to-all-start.1 = ((bf16[16,32,512]{2,1,0:T(8,128)(2,1)}), bf16[16,32,512]{2,1,0:T(8,128)(2,1)S(1)}, u32[]{:S(2)}, u32[]{:S(2)}) async-start(bf16[16,32,512]{2,1,0:T(8,128)(2,1)} %get-tuple-element.15), calls=%async_computation.1 | async-start | bytes 1048576 | tf_op jit(solution)/shard_map/all_to_all | solution.py:44
  83.4 0.6 gather_fusion.3
  84.0 0.6 gather_fusion.7
  84.5 0.6 gather_fusion.9
  85.1 12.2 %all-to-all-done.1 = bf16[16,32,512]{2,1,0:T(8,128)(2,1)S(1)} async-done(((bf16[16,32,512]{2,1,0:T(8,128)(2,1)}), bf16[16,32,512]{2,1,0:T(8,128)(2,1)S(1)}, u32[]{:S(2)}, u32[]{:S(2)}) %all-to-all-start.1) | async-done | bytes 524320 | tf_op jit(solution)/shard_map/all_to_all | solution.py:44
  97.3 0.6 gather_fusion.5
  98.9 0.6 fusion.23
  99.5 0.9 convolution_convert_fusion
  101.5 0.5 fusion.24
  101.9 0.7 copy-done.4
  102.7 0.5 convolution_add_fusion.1
  103.2 0.7 copy-done.5
  103.9 1.3 fusion.6
  105.4 14.1 %reduce-scatter.2.cloned.1.call-done = bf16[512,256]{0,1:T(8,128)(2,1)} async-done(((bf16[1024,256]{0,1:T(8,128)(2,1)}), bf16[512,256]{0,1:T(8,128)(2,1)}) %reduce-scatter.2.cloned.1.call-update) | async-done | bytes 262160 | tf_op jit(solution)/shard_map/reduce_scatter | solution.py:119
  119.5 1.5 %gather_fusion = bf16[16,512,32]{1,2,0:T(8,128)(2,1)S(1)} fusion(bf16[512,8,32]{0,2,1:T(8,128)(2,1)} %bitcast.45, s32[1024]{0:T(1024)S(1)} %pad_clamp_fusion.1), kind=kCustom, calls=%fused_computation.8 | custom fusion | bytes 1048640 | tf_op jit(solution)/shard_map/jit(_take)/gather | solution.py:123
  121.0 0.9 select_bitcast_fusion
  122.0 5.6 %all-to-all-start.4 = ((bf16[512,16,32]{0,2,1:T(8,128)(2,1)}), bf16[512,16,32]{0,2,1:T(8,128)(2,1)S(1)}, u32[]{:S(2)}, u32[]{:S(2)}) async-start(bf16[512,16,32]{0,2,1:T(8,128)(2,1)} %select_bitcast_fusion), calls=%async_computation.5 | async-start | bytes 1048576 | tf_op jit(solution)/shard_map/all_to_all | solution.py:125
  127.8 14.1 %all-to-all-done.4 = bf16[512,16,32]{0,2,1:T(8,128)(2,1)S(1)} async-done(((bf16[512,16,32]{0,2,1:T(8,128)(2,1)}), bf16[512,16,32]{0,2,1:T(8,128)(2,1)S(1)}, u32[]{:S(2)}, u32[]{:S(2)}) %all-to-all-start.4) | async-done | bytes 524320 | tf_op jit(solution)/shard_map/all_to_all | solution.py:125
  141.9 0.6 gather_fusion.1
  142.4 0.8 bitcast_select_fusion
  (55 shorter events, 3.8 us)
Async XLA Ops:
  6.5 94.9 %copy-start = (bf16[1024,512]{1,0:T(8,128)(2,1)S(1)}, bf16[1024,512]{1,0:T(8,128)(2,1)}, u32[]{:S(2)}) copy-start(bf16[1024,512]{1,0:T(8,128)(2,1)} %param.17) | copy-start | bytes 3145732
  16.3 2.4 %copy-start.1 = (bf16[192,512]{1,0:T(8,128)(2,1)S(1)}, bf16[192,512]{1,0:T(8,128)(2,1)}, u32[]{:S(2)}) copy-start(bf16[192,512]{1,0:T(8,128)(2,1)} %param.14) | copy-start | bytes 589828
  18.1 1.2 copy-start.2
  18.7 1.2 copy-start.3
  42.0 22.5 %copy-start.6 = (s32[96]{0:T(128)S(1)}, s32[96]{0:T(128)}, u32[]{:S(2)}) copy-start(s32[96]{0:T(128)} %param.21) | copy-start | bytes 1156
  60.4 18.4 %all-to-all-start.3 = ((bf16[16,32,512]{2,1,0:T(8,128)(2,1)}), bf16[16,32,512]{2,1,0:T(8,128)(2,1)S(1)}, u32[]{:S(2)}, u32[]{:S(2)}) async-start(bf16[16,32,512]{2,1,0:T(8,128)(2,1)} %get-tuple-element.17), calls=%async_computation.3 | async-start | bytes 1048576 | tf_op jit(solution)/shard_map/all_to_all | solution.py:46
  78.8 18.4 %all-to-all-start.1 = ((bf16[16,32,512]{2,1,0:T(8,128)(2,1)}), bf16[16,32,512]{2,1,0:T(8,128)(2,1)S(1)}, u32[]{:S(2)}, u32[]{:S(2)}) async-start(bf16[16,32,512]{2,1,0:T(8,128)(2,1)} %get-tuple-element.15), calls=%async_computation.1 | async-start | bytes 1048576 | tf_op jit(solution)/shard_map/all_to_all | solution.py:44
  83.0 36.5 %reduce-scatter.2.cloned.1.call-start = ((), (), s32[]{:S(2)}) async-start(), calls=%async_computation.6 | async-start | bytes 786432 | tf_op jit(solution)/shard_map/reduce_scatter | solution.py:119
  101.4 1.2 copy-start.4
  102.7 1.2 copy-start.5
  122.0 19.9 %all-to-all-start.4 = ((bf16[512,16,32]{0,2,1:T(8,128)(2,1)}), bf16[512,16,32]{0,2,1:T(8,128)(2,1)S(1)}, u32[]{:S(2)}, u32[]{:S(2)}) async-start(bf16[512,16,32]{0,2,1:T(8,128)(2,1)} %select_bitcast_fusion), calls=%async_computation.5 | async-start | bytes 1048576 | tf_op jit(solution)/shard_map/all_to_all | solution.py:125
Sparse Core Ops, SparseCore 0:
  105.3 14.1 reduce-scatter.1
where the time goes:
time: 151 us; the launch traced here: 150 us
  waiting for transfers between devices  53.8 us (36%)
  blocking collectives  47.3 us (31%)
  starting transfers between devices  14 us (9%)
  between operations  13.7 us (9%)
  local copies, waits for them, and re-layouts  9.34 us (6%)
  matrix products  6.38 us (4%)
  other arithmetic  5.46 us (4%)
    all_to_all x1, blocking collectives, per_device(): lax.all_to_all(outgoing(keys), 'tok', split_axis=0, concat_axis=0, tiled=...  20.2 us
    all_to_all x1, blocking collectives, per_device(): lax.all_to_all(outgoing(grad_heads), 'tok', split_axis=0, concat_axis=0,...  18.4 us
    all_to_all x1, waiting for transfers between devices, per_device(): lax.all_to_all(picked, 'tok', split_axis=1, concat_axis=1, tiled=True)  14.1 us
    reduce_scatter x1, waiting for transfers between devices, per_device(): lax.psum_scatter(total.astype(jnp.bfloat16), 'head', scatter_dimension=0,...  14.1 us
    all_to_all x1, waiting for transfers between devices, per_device(): lax.all_to_all(outgoing(values), 'tok', split_axis=0, concat_axis=0, tile...  13.4 us
    all_to_all x1, waiting for transfers between devices, per_device(): lax.all_to_all(outgoing(queries), 'tok', split_axis=0, concat_axis=0, til...  12.2 us
    all_gather x1, blocking collectives, per_device(): lax.all_gather(out_grad, 'head', axis=1, tiled=True)  8.79 us
    all_to_all x1, starting transfers between devices, per_device(): lax.all_to_all(picked, 'tok', split_axis=1, concat_axis=1, tiled=True)  5.62 us
  transfers between devices with their start and end apart: 4, of which 4 were waited for; matrix products, arithmetic and copies ran while one was open for 2% of the time, Pallas kernels for 0%

commit v1 on v0

--- a/solution.py
+++ b/solution.py
@@ -122,7 +122,10 @@
     column_share = column_share.reshape(share_rows, slot_count, PAGE)
     picked = jnp.take(column_share, back_slot, axis=1)
     picked = jnp.where(back_any[None, :, None], picked, jnp.zeros_like(picked))
-    returned = lax.all_to_all(picked, "tok", split_axis=1, concat_axis=1, tiled=True)
+    returned = jnp.concatenate(
+        lax.all_to_all(jnp.stack(jnp.split(picked, lax.axis_size("tok"), axis=1)), "tok", 0, 0),
+        axis=1,
+    )
     input_grad = jnp.take(returned, my_clusters, axis=1).reshape(share_rows, tok_rows).T
     return input_grad
 

time: 151 us -> 160 us (1.060)
  local copies, waits for them, and re-layouts: 9.34 us -> 19 us
    unnamed x14 -> x29, local copies, waits for them, and re-layouts: 1.48 us -> 10.6 us
where the time goes in v1:
time: 160 us; the launch traced here: 159 us
  waiting for transfers between devices  53.8 us (34%)
  blocking collectives  47.3 us (30%)
  local copies, waits for them, and re-layouts  19 us (12%)
  starting transfers between devices  14 us (9%)
  between operations  13.7 us (9%)
  matrix products  6.38 us (4%)
  other arithmetic  4.67 us (3%)
    all_to_all x1, blocking collectives, per_device(): lax.all_to_all(outgoing(keys), 'tok', split_axis=0, concat_axis=0, tiled=...  20.2 us
    all_to_all x1, blocking collectives, per_device(): lax.all_to_all(outgoing(grad_heads), 'tok', split_axis=0, concat_axis=0,...  18.4 us
    all_to_all x1, waiting for transfers between devices, per_device(): lax.all_to_all(jnp.stack(jnp.split(picked, lax.axis_size('tok'), axis=1))...  14.1 us
    reduce_scatter x1, waiting for transfers between devices, per_device(): lax.psum_scatter(total.astype(jnp.bfloat16), 'head', scatter_dimension=0,...  14.1 us
    all_to_all x1, waiting for transfers between devices, per_device(): lax.all_to_all(outgoing(values), 'tok', split_axis=0, concat_axis=0, tile...  13.4 us
    all_to_all x1, waiting for transfers between devices, per_device(): lax.all_to_all(outgoing(queries), 'tok', split_axis=0, concat_axis=0, til...  12.2 us
    unnamed x29, local copies, waits for them, and re-layouts  10.6 us
    all_gather x1, blocking collectives, per_device(): lax.all_gather(out_grad, 'head', axis=1, tiled=True)  8.79 us
  transfers between devices with their start and end apart: 4, of which 4 were waited for; matrix products, arithmetic and copies ran while one was open for 2% of the time, Pallas kernels for 0%

profile of v1, /device:TPU:0, one launch (start us, length us, event | category | flops | bytes accessed | tf_op | source)
XLA Modules:
  0.0 158.9 jit_solution(12673336185960434590)
XLA Ops:
  6.5 0.8 compare_and_fusion.3
  7.6 8.8 %all_gather.3 = bf16[192,1024]{1,0:T(8,128)(2,1)S(1)} all-gather(bf16[192,512]{1,0:T(8,128)(2,1)} %param.16), channel_id=1, replica_groups=mesh['head'=2,'tok'=16] {'head'}, dimensions={1}, use_global_device_ids=true | all-gather | bytes 589824 | tf_op jit(solution)/shard_map/all_gather | solution.py:22
  16.3 1.8 %convolution_convert_fusion.1 = bf16[192,512]{1,0:T(8,128)(2,1)S(1)} fusion(bf16[192,1024]{1,0:T(8,128)(2,1)S(1)} %all_gather.3, bf16[512,1024]{1,0:T(8,128)(2,1)} %param.20), kind=kOutput, calls=%fused_computation.25 | convolution fusion | flops 201424896 | bytes 1638400 | tf_op jit(solution)/shard_map/td,hd->th/dot_general | solution.py:20
  20.5 1.3 select_select_fusion.2
  21.8 20.2 %all_to_all.25 = bf16[16,32,512]{2,1,0:T(8,128)(2,1)S(1)} all-to-all(bf16[16,32,512]{2,1,0:T(8,128)(2,1)S(1)} %get-tuple-element.18), channel_id=1, replica_groups=mesh['head'=2,'tok'=16] {'tok'}, dimensions={0} | all-to-all | bytes 1048576 | tf_op jit(solution)/shard_map/all_to_all | solution.py:45
  42.0 18.4 %all_to_all.26 = bf16[16,32,512]{2,1,0:T(8,128)(2,1)S(1)} all-to-all(bf16[16,32,512]{2,1,0:T(8,128)(2,1)S(1)} %get-tuple-element.16), channel_id=1, replica_groups=mesh['head'=2,'tok'=16] {'tok'}, dimensions={0} | all-to-all | bytes 1048576 | tf_op jit(solution)/shard_map/all_to_all | solution.py:47
  60.4 4.2 %all-to-all-start.3 = ((bf16[16,32,512]{2,1,0:T(8,128)(2,1)}), bf16[16,32,512]{2,1,0:T(8,128)(2,1)S(1)}, u32[]{:S(2)}, u32[]{:S(2)}) async-start(bf16[16,32,512]{2,1,0:T(8,128)(2,1)} %get-tuple-element.17), calls=%async_computation.3 | async-start | bytes 1048576 | tf_op jit(solution)/shard_map/all_to_all | solution.py:46
  65.4 13.4 %all-to-all-done.3 = bf16[16,32,512]{2,1,0:T(8,128)(2,1)S(1)} async-done(((bf16[16,32,512]{2,1,0:T(8,128)(2,1)}), bf16[16,32,512]{2,1,0:T(8,128)(2,1)S(1)}, u32[]{:S(2)}, u32[]{:S(2)}) %all-to-all-start.3) | async-done | bytes 524320 | tf_op jit(solution)/shard_map/all_to_all | solution.py:46
  78.8 4.2 %all-to-all-start.1 = ((bf16[16,32,512]{2,1,0:T(8,128)(2,1)}), bf16[16,32,512]{2,1,0:T(8,128)(2,1)S(1)}, u32[]{:S(2)}, u32[]{:S(2)}) async-start(bf16[16,32,512]{2,1,0:T(8,128)(2,1)} %get-tuple-element.15), calls=%async_computation.1 | async-start | bytes 1048576 | tf_op jit(solution)/shard_map/all_to_all | solution.py:44
  85.1 12.2 %all-to-all-done.1 = bf16[16,32,512]{2,1,0:T(8,128)(2,1)S(1)} async-done(((bf16[16,32,512]{2,1,0:T(8,128)(2,1)}), bf16[16,32,512]{2,1,0:T(8,128)(2,1)S(1)}, u32[]{:S(2)}, u32[]{:S(2)}) %all-to-all-start.1) | async-done | bytes 524320 | tf_op jit(solution)/shard_map/all_to_all | solution.py:44
  98.9 0.6 fusion.39
  99.5 0.9 convolution_convert_fusion
  101.9 0.7 copy-done.4
  103.2 0.7 copy-done.5
  103.9 1.3 fusion.6
  105.4 14.1 %reduce-scatter.2.cloned.1.call-done = bf16[512,256]{0,1:T(8,128)(2,1)} async-done(((bf16[1024,256]{0,1:T(8,128)(2,1)}), bf16[512,256]{0,1:T(8,128)(2,1)}) %reduce-scatter.2.cloned.1.call-update) | async-done | bytes 262160 | tf_op jit(solution)/shard_map/reduce_scatter | solution.py:119
  119.5 1.5 gather_fusion
  121.2 0.6 fusion.29
  121.8 0.6 fusion.28
  123.0 0.6 fusion.26
  124.2 0.6 fusion.24
  125.4 0.6 fusion.22
  126.6 0.6 fusion.20
  127.2 0.6 fusion.19
  127.8 0.6 fusion.18
  128.4 0.6 fusion.17
  129.0 0.6 fusion.16
  129.7 0.6 fusion.15
  130.3 0.6 fusion.14
  130.9 5.6 %all-to-all-start.4 = ((bf16[16,512,1,32]{1,3,2,0:T(8,128)(2,1)}), bf16[16,512,1,32]{1,3,2,0:T(8,128)(2,1)S(1)}, u32[]{:S(2)}, u32[]{:S(2)}) async-start(bf16[16,512,1,32]{1,3,2,0:T(8,128)(2,1)} %fusion.14), calls=%async_computation.5 | async-start | bytes 1048576 | tf_op jit(solution)/shard_map/all_to_all | solution.py:126
  136.7 14.1 %all-to-all-done.4 = bf16[16,512,1,32]{1,3,2,0:T(8,128)(2,1)S(1)} async-done(((bf16[16,512,1,32]{1,3,2,0:T(8,128)(2,1)}), bf16[16,512,1,32]{1,3,2,0:T(8,128)(2,1)S(1)}, u32[]{:S(2)}, u32[]{:S(2)}) %all-to-all-start.4) | async-done | bytes 524320 | tf_op jit(solution)/shard_map/all_to_all | solution.py:126
  151.3 0.8 bitcast_select_fusion
  (71 shorter events, 12.4 us)
Async XLA Ops:
  6.5 94.9 %copy-start = (bf16[1024,512]{1,0:T(8,128)(2,1)S(1)}, bf16[1024,512]{1,0:T(8,128)(2,1)}, u32[]{:S(2)}) copy-start(bf16[1024,512]{1,0:T(8,128)(2,1)} %param.17) | copy-start | bytes 3145732
  16.3 2.4 %copy-start.1 = (bf16[192,512]{1,0:T(8,128)(2,1)S(1)}, bf16[192,512]{1,0:T(8,128)(2,1)}, u32[]{:S(2)}) copy-start(bf16[192,512]{1,0:T(8,128)(2,1)} %param.14) | copy-start | bytes 589828
  18.1 1.2 copy-start.2
  18.7 1.2 copy-start.3
  42.0 22.5 %copy-start.6 = (s32[96]{0:T(128)S(1)}, s32[96]{0:T(128)}, u32[]{:S(2)}) copy-start(s32[96]{0:T(128)} %param.21) | copy-start | bytes 1156
  60.4 18.4 %all-to-all-start.3 = ((bf16[16,32,512]{2,1,0:T(8,128)(2,1)}), bf16[16,32,512]{2,1,0:T(8,128)(2,1)S(1)}, u32[]{:S(2)}, u32[]{:S(2)}) async-start(bf16[16,32,512]{2,1,0:T(8,128)(2,1)} %get-tuple-element.17), calls=%async_computation.3 | async-start | bytes 1048576 | tf_op jit(solution)/shard_map/all_to_all | solution.py:46
  78.8 18.4 %all-to-all-start.1 = ((bf16[16,32,512]{2,1,0:T(8,128)(2,1)}), bf16[16,32,512]{2,1,0:T(8,128)(2,1)S(1)}, u32[]{:S(2)}, u32[]{:S(2)}) async-start(bf16[16,32,512]{2,1,0:T(8,128)(2,1)} %get-tuple-element.15), calls=%async_computation.1 | async-start | bytes 1048576 | tf_op jit(solution)/shard_map/all_to_all | solution.py:44
  83.0 36.5 %reduce-scatter.2.cloned.1.call-start = ((), (), s32[]{:S(2)}) async-start(), calls=%async_computation.6 | async-start | bytes 786432 | tf_op jit(solution)/shard_map/reduce_scatter | solution.py:119
  101.4 1.2 copy-start.4
  102.7 1.2 copy-start.5
  130.9 19.9 %all-to-all-start.4 = ((bf16[16,512,1,32]{1,3,2,0:T(8,128)(2,1)}), bf16[16,512,1,32]{1,3,2,0:T(8,128)(2,1)S(1)}, u32[]{:S(2)}, u32[]{:S(2)}) async-start(bf16[16,512,1,32]{1,3,2,0:T(8,128)(2,1)} %fusion.14), calls=%async_computation.5 | async-start | bytes 1048576 | tf_op jit(solution)/shard_map/all_to_all | solution.py:126
Sparse Core Ops, SparseCore 0:
  105.3 14.1 reduce-scatter.1
